TPU v7x, 32 devices: a whole 2x2x4 slice. The times are simulated.
32 devices in a mesh: pipe: 4 (over y, x), dp: 4 (over z), tensor: 2 (over core).
Axes of the slice: x: 2, y: 2, z: 4, core: 2. Of those that a mesh axis runs over, the one named last changes fastest.
Arguments:
- llm_grad: bfloat16 [4, 128, 1664], P(None, 'dp'), may hold values from -6 to 6
- slot_row: int32 [4, 4, 32], P(None, 'dp'), may hold values from 0 to 31, each once within a row
- counts: int32 [4, 4], P('dp'), may hold values from 8 to 32, as said below
- saved_in: bfloat16 [4, 4, 128, 1664], P('pipe', None, 'dp'), may hold values from -6 to 6
- saved_pre: bfloat16 [4, 4, 128, 6400], P('pipe', None, 'dp', 'tensor'), may hold values from -6 to 6
- weights: bfloat16 [4, 1664, 6400], P('pipe', 'dp', 'tensor'), may hold values from -0.15625 to 0.15625
- channel_scale: float32 [4, 1664], P('pipe'), may hold values from 0.25 to 2
Outputs:
- weight_grad: bfloat16 [4, 1664, 6400], P('pipe', 'dp', 'tensor')
- section_grad: bfloat16 [4, 4, 128, 1664], P('pipe', None, 'dp')
Inputs may be any that keep to these rules, and one draw needn't show every extreme that they name: For each micro-batch and rank, slot_row lists every row of the rank once. `counts`: both ends of the range occur in every draw.
All inputs are finite; a program needn't handle non-finite values.
Results may differ from a plain program's by a relative error of at most 0.023.
Values may be sent and summed in bfloat16 or wider, within the bound.
No kernel may reach another device: no remote copies, remote signals or barrier semaphores. Data moves between devices by JAX's collectives and lax.ppermute only.
A program may use at most 128 MiB of HBM per device.

v0:
```python
import jax
import jax.numpy as jnp
from jax import lax
from jax.sharding import PartitionSpec as P

norm_eps = 1e-06
root_half = 0.7071067811865476
inv_root_two_pi = 0.3989422804014327


def shortened(value):

    def short(part):
        return part.astype(jnp.bfloat16) if part.dtype == jnp.float32 else part

    return jax.tree.map(short, value)


def shifted(block, axis, distance):
    devices = range(lax.axis_size(axis))
    route = [(i - distance, i) for i in devices if i - distance in devices]
    return lax.ppermute(block, axis, route)


def gelu_parts(pre_act):
    normal_cdf = 0.5 * (1.0 + jax.scipy.special.erf(pre_act * root_half))
    density = jnp.exp(-0.5 * pre_act * pre_act) * inv_root_two_pi
    return (pre_act * normal_cdf, normal_cdf + pre_act * density)


def local_top(llm_grad, slot_row, counts):
    row_count = llm_grad.shape[1]
    slot_ids = jnp.arange(row_count, dtype=jnp.int32)
    kept_mask = slot_ids[None, :] < counts[:, None]
    source = jnp.where(kept_mask[..., None], llm_grad, jnp.zeros_like(llm_grad))
    onehot = (slot_row[:, :, None] == slot_ids[None, None, :]).astype(jnp.bfloat16)
    placed = jnp.einsum("mjr,mjd->mrd", onehot, source, preferred_element_type=jnp.float32)
    return placed.astype(jnp.bfloat16)


def norm_back(incoming, dnorm, unit_rows, inv_std, channel_gain):
    scaled_back = dnorm * channel_gain
    back = inv_std * (
        scaled_back
        - jnp.mean(scaled_back, axis=-1, keepdims=True)
        - unit_rows * jnp.mean(scaled_back * unit_rows, axis=-1, keepdims=True)
    )
    return (incoming.astype(jnp.float32) + back).astype(jnp.bfloat16)


def body(llm_grad, slot_row, counts, saved_in, saved_pre, weights, channel_scale):
    sections = lax.axis_size("pipe")
    section_index = lax.axis_index("pipe")
    micro_count = llm_grad.shape[0]
    row_count = llm_grad.shape[1]
    model_width = llm_grad.shape[2]
    hidden = saved_pre.shape[3]
    is_up = section_index % 2 == 0
    is_top = section_index == sections - 1
    full_weight = lax.all_gather(weights[0], "dp", axis=0, tiled=True)
    channel_gain = channel_scale[0]
    top_grad = local_top(llm_grad, slot_row[:, 0], counts[0])
    zero_wide = jnp.zeros((row_count, model_width), jnp.float32)
    zero_narrow = jnp.zeros((row_count, model_width), jnp.bfloat16)
    zero_hidden = jnp.zeros((row_count, hidden), jnp.bfloat16)

    def spare_work(incoming, hidden_in, inputs, pre_act):
        return (zero_wide, zero_hidden, zero_narrow, zero_hidden)

    def down_work(incoming, hidden_in, inputs, pre_act):
        scaled = (incoming.astype(jnp.float32) * channel_gain).astype(jnp.bfloat16)
        hidden_grad = jnp.dot(scaled, full_weight, preferred_element_type=jnp.float32).astype(
            jnp.bfloat16
        )
        activated = gelu_parts(pre_act.astype(jnp.float32))[0].astype(jnp.bfloat16)
        return (zero_wide, hidden_grad, scaled, activated)

    def up_work(incoming, hidden_in, inputs, pre_act):
        act_grad = (
            hidden_in.astype(jnp.float32) * gelu_parts(pre_act.astype(jnp.float32))[1]
        ).astype(jnp.bfloat16)
        values = inputs.astype(jnp.float32)
        center = values - jnp.mean(values, axis=-1, keepdims=True)
        inv_std = lax.rsqrt(jnp.mean(center * center, axis=-1, keepdims=True) + norm_eps)
        normed = (center * inv_std * channel_gain).astype(jnp.bfloat16)
        partial_value = lax.dot_general(
            act_grad, full_weight, (((1,), (1,)), ((), ())), preferred_element_type=jnp.float32
        )
        return (partial_value, zero_hidden, normed, act_grad)

    def advance(loop_state, tick_index):
        grad_store, out_buffer, recv_hidden, recv_res = loop_state
        micro_index = tick_index - (sections - 1 - section_index)
        is_valid = (micro_index >= 0) & (micro_index < micro_count)
        micro_safe = jnp.clip(micro_index, 0, micro_count - 1)
        incoming = jnp.where(is_top, top_grad[micro_safe], recv_res)
        inputs = saved_in[0, micro_safe]
        pre_act = saved_pre[0, micro_safe]
        branch = jnp.where(is_valid, jnp.where(is_up, 2, 1), 0).astype(jnp.int32)
        partial_value, hidden_out, left_side, right_side = lax.switch(
            branch, [spare_work, down_work, up_work], incoming, recv_hidden, inputs, pre_act
        )
        values = inputs.astype(jnp.float32)
        center = values - jnp.mean(values, axis=-1, keepdims=True)
        inv_std = lax.rsqrt(jnp.mean(center * center, axis=-1, keepdims=True) + norm_eps)
        unit_rows = center * inv_std
        summed = jax.tree.map(
            lambda part: part.astype(jnp.float32), lax.psum(shortened(partial_value), "tensor")
        )
        back_out = norm_back(incoming, summed, unit_rows, inv_std, channel_gain)
        outgoing = jnp.where(is_up, back_out, incoming)
        write_at = jnp.where(is_valid, micro_safe, micro_count)
        out_buffer = lax.dynamic_update_index_in_dim(out_buffer, outgoing, write_at, 0)
        left_buffer, right_buffer = grad_store
        left_buffer = lax.dynamic_update_index_in_dim(left_buffer, left_side, write_at, 0)
        right_buffer = lax.dynamic_update_index_in_dim(right_buffer, right_side, write_at, 0)
        grad_store = (left_buffer, right_buffer)
        recv_hidden, recv_res = (
            shifted(shortened(hidden_out), "pipe", -1).astype(hidden_out.dtype),
            shifted(outgoing, "pipe", -1),
        )
        return ((grad_store, out_buffer, recv_hidden, recv_res), None)

    grad_store = (
        jnp.zeros((micro_count + 1, row_count, model_width), jnp.bfloat16),
        jnp.zeros((micro_count + 1, row_count, hidden), jnp.bfloat16),
    )
    out_buffer = jnp.zeros((micro_count + 1, row_count, model_width), jnp.bfloat16)
    tick_count = micro_count + sections - 1
    loop_state = (grad_store, out_buffer, zero_hidden, zero_narrow)
    loop_state, unused = lax.scan(advance, loop_state, jnp.arange(tick_count, dtype=jnp.int32))
    grad_store, out_buffer, recv_hidden, recv_res = loop_state
    left_buffer, right_buffer = grad_store
    flat_left = left_buffer[:micro_count].reshape(micro_count * row_count, model_width)
    flat_right = right_buffer[:micro_count].reshape(micro_count * row_count, hidden)
    weight_out = lax.psum_scatter(
        lax.dot_general(
            flat_left, flat_right, (((0,), (0,)), ((), ())), preferred_element_type=jnp.float32
        ).astype(jnp.bfloat16),
        "dp",
        scatter_dimension=0,
        tiled=True,
    )
    return (weight_out[None], out_buffer[:micro_count][None])


def solution(mesh):
    in_specs = (
        P(None, "dp", None),
        P(None, "dp", None),
        P("dp", None),
        P("pipe", None, "dp", None),
        P("pipe", None, "dp", "tensor"),
        P("pipe", "dp", "tensor"),
        P("pipe", None),
    )
    out_specs = (P("pipe", "dp", "tensor"), P("pipe", None, "dp", None))
    return jax.shard_map(body, mesh=mesh, in_specs=in_specs, out_specs=out_specs, check_vma=False)
```

profile of v0, /device:TPU:0, one launch (start us, length us, event | category | flops | bytes accessed | tf_op | source)
XLA Modules:
  0.0 668.3 jit_solution(7804911929858855091)
XLA Ops:
  8.6 1.4 convolution_convert_fusion.1
  10.0 188.9 %all-gather.3.cloned.1.call-done = bf16[1,1664,3200]{2,1,0:T(8,128)(2,1)} async-done(((bf16[1,416,3200]{2,1,0:T(8,128)(2,1)}), bf16[1,1664,3200]{2,1,0:T(8,128)(2,1)}) %all-gather.3.cloned.1.call-update) | async-done | bytes 10649616 | tf_op jit(solution)/shard_map/all_gather | solution.py:60
  199.9 271.5 %while.20 = (s32[]{:T(128)}, bf16[5,32,1664]{2,1,0:T(8,128)(2,1)}, bf16[5,32,3200]{2,1,0:T(8,128)(2,1)S(1)}, bf16[5,32,1664]{2,1,0:T(8,128)(2,1)S(1)}, bf16[32,3...) while((s32[]{:T(128)}, bf16[5,32,1664]{2,1,0:T(8,128)(2,1)}, ...), condition=%wide.region_11.12_spmd, body=%wide.region_0.11_spmd.sunk | while | flops 345374784 | bytes 17218160 | solution.py:131
  201.2 1.0 convert_reduce_fusion.3
  202.2 1.0 dynamic-slice_bitcast_fusion.4
  204.0 1.3 collective-permute-start
  206.3 20.6 %all-reduce.2.cloned.1.call-done = bf16[32,1664]{1,0:T(8,128)(2,1)} async-done(((bf16[32,1664]{1,0:T(8,128)(2,1)}), bf16[32,1664]{1,0:T(8,128)(2,1)}) %all-reduce.2.cloned.1.call-update) | async-done | bytes 106512 | tf_op jit(solution)/shard_map/while/body/eval_jaxpr/psum | solution.py:108
  226.9 1.1 fusion.48
  228.0 1.1 bitcast_dynamic-update-slice_fusion.2
  229.1 1.3 collective-permute-start.1
  231.0 5.2 collective-permute-done.1
  237.4 1.0 convert_reduce_fusion.3
  238.4 1.0 dynamic-slice_bitcast_fusion.4
  240.2 1.3 collective-permute-start
  242.5 23.8 %all-reduce.2.cloned.1.call-done = bf16[32,1664]{1,0:T(8,128)(2,1)} async-done(((bf16[32,1664]{1,0:T(8,128)(2,1)}), bf16[32,1664]{1,0:T(8,128)(2,1)}) %all-reduce.2.cloned.1.call-update) | async-done | bytes 106512 | tf_op jit(solution)/shard_map/while/body/eval_jaxpr/psum | solution.py:108
  266.2 1.1 fusion.48
  267.4 1.1 bitcast_dynamic-update-slice_fusion.2
  268.4 1.3 collective-permute-start.1
  270.4 5.2 collective-permute-done.1
  276.8 1.0 convert_reduce_fusion.3
  279.6 1.3 collective-permute-start
  281.9 23.8 %all-reduce.2.cloned.1.call-done = bf16[32,1664]{1,0:T(8,128)(2,1)} async-done(((bf16[32,1664]{1,0:T(8,128)(2,1)}), bf16[32,1664]{1,0:T(8,128)(2,1)}) %all-reduce.2.cloned.1.call-update) | async-done | bytes 106512 | tf_op jit(solution)/shard_map/while/body/eval_jaxpr/psum | solution.py:108
  305.6 1.1 fusion.48
  306.8 1.1 bitcast_dynamic-update-slice_fusion.2
  307.8 1.3 collective-permute-start.1
  309.8 5.2 collective-permute-done.1
  316.2 1.0 convert_reduce_fusion.3
  318.2 7.9 %conditional.2 = (bf16[32,1664]{1,0:T(8,128)(2,1)S(1)}, bf16[32,3200]{1,0:T(8,128)(2,1)S(1)}, bf16[1,32,1664]{2,1,0:T(8,128)(2,1)S(1)}, bf16[1,32,3200]{2,1,0:T(8,128)(2,1)S(1)}) conditional(s32[]{:T(128)} %clamp.6, () %tuple.62, (bf16[32,1664]{1,0:T(8,128)(2,1)S(1)}, f32[1,1664]{1,0:T(1,128)}, bf16[1664,3200]{1,0:T(8,128)(2,1)}, ...), branch_computations={%region_1.1_spmd, %region_2.2_spmd, %region_3.5_spmd} | conditional | flops 343830560 | bytes 12458690 | solution.py:100
  318.2 7.1 %fusion.21 = bf16[32,1664]{1,0:T(8,128)(2,1)S(1)} fusion(bf16[1664,3200]{1,0:T(8,128)(2,1)} %get-tuple-element.187, bf16[32,3200]{1,0:T(8,128)(2,1)S(1)} %get-tuple-element.186, bf16[32,3200]{1,0:T(8,128)(2,1)S(1)} %get-tuple-element.185), kind=kOutput, calls=%fused_computation.33 | convolution fusion | flops 342016000 | bytes 11165696 | tf_op jit(solution)/shard_map/while/body/eval_jaxpr/cond/branch_2_fun/dot_general | solution.py:86
  326.8 1.3 collective-permute-start
  329.1 15.9 %all-reduce.2.cloned.1.call-done = bf16[32,1664]{1,0:T(8,128)(2,1)} async-done(((bf16[32,1664]{1,0:T(8,128)(2,1)}), bf16[32,1664]{1,0:T(8,128)(2,1)}) %all-reduce.2.cloned.1.call-update) | async-done | bytes 106512 | tf_op jit(solution)/shard_map/while/body/eval_jaxpr/psum | solution.py:108
  345.0 1.1 fusion.48
  346.1 1.1 bitcast_dynamic-update-slice_fusion.2
  347.2 1.3 collective-permute-start.1
  349.2 5.2 collective-permute-done.1
  355.6 1.0 convert_reduce_fusion.3
  357.6 7.9 %conditional.2 = (bf16[32,1664]{1,0:T(8,128)(2,1)S(1)}, bf16[32,3200]{1,0:T(8,128)(2,1)S(1)}, bf16[1,32,1664]{2,1,0:T(8,128)(2,1)S(1)}, bf16[1,32,3200]{2,1,0:T(8,128)(2,1)S(1)}) conditional(s32[]{:T(128)} %clamp.6, () %tuple.62, (bf16[32,1664]{1,0:T(8,128)(2,1)S(1)}, f32[1,1664]{1,0:T(1,128)}, bf16[1664,3200]{1,0:T(8,128)(2,1)}, ...), branch_computations={%region_1.1_spmd, %region_2.2_spmd, %region_3.5_spmd} | conditional | flops 343830560 | bytes 12458690 | solution.py:100
  357.6 7.1 %fusion.21 = bf16[32,1664]{1,0:T(8,128)(2,1)S(1)} fusion(bf16[1664,3200]{1,0:T(8,128)(2,1)} %get-tuple-element.187, bf16[32,3200]{1,0:T(8,128)(2,1)S(1)} %get-tuple-element.186, bf16[32,3200]{1,0:T(8,128)(2,1)S(1)} %get-tuple-element.185), kind=kOutput, calls=%fused_computation.33 | convolution fusion | flops 342016000 | bytes 11165696 | tf_op jit(solution)/shard_map/while/body/eval_jaxpr/cond/branch_2_fun/dot_general | solution.py:86
  366.2 1.3 collective-permute-start
  368.5 15.9 %all-reduce.2.cloned.1.call-done = bf16[32,1664]{1,0:T(8,128)(2,1)} async-done(((bf16[32,1664]{1,0:T(8,128)(2,1)}), bf16[32,1664]{1,0:T(8,128)(2,1)}) %all-reduce.2.cloned.1.call-update) | async-done | bytes 106512 | tf_op jit(solution)/shard_map/while/body/eval_jaxpr/psum | solution.py:108
  384.4 1.1 fusion.48
  385.5 1.1 bitcast_dynamic-update-slice_fusion.2
  386.6 1.3 collective-permute-start.1
  388.6 5.2 collective-permute-done.1
  395.0 1.0 convert_reduce_fusion.3
  397.0 7.9 %conditional.2 = (bf16[32,1664]{1,0:T(8,128)(2,1)S(1)}, bf16[32,3200]{1,0:T(8,128)(2,1)S(1)}, bf16[1,32,1664]{2,1,0:T(8,128)(2,1)S(1)}, bf16[1,32,3200]{2,1,0:T(8,128)(2,1)S(1)}) conditional(s32[]{:T(128)} %clamp.6, () %tuple.62, (bf16[32,1664]{1,0:T(8,128)(2,1)S(1)}, f32[1,1664]{1,0:T(1,128)}, bf16[1664,3200]{1,0:T(8,128)(2,1)}, ...), branch_computations={%region_1.1_spmd, %region_2.2_spmd, %region_3.5_spmd} | conditional | flops 343830560 | bytes 12458690 | solution.py:100
  397.0 7.1 %fusion.21 = bf16[32,1664]{1,0:T(8,128)(2,1)S(1)} fusion(bf16[1664,3200]{1,0:T(8,128)(2,1)} %get-tuple-element.187, bf16[32,3200]{1,0:T(8,128)(2,1)S(1)} %get-tuple-element.186, bf16[32,3200]{1,0:T(8,128)(2,1)S(1)} %get-tuple-element.185), kind=kOutput, calls=%fused_computation.33 | convolution fusion | flops 342016000 | bytes 11165696 | tf_op jit(solution)/shard_map/while/body/eval_jaxpr/cond/branch_2_fun/dot_general | solution.py:86
  405.6 1.3 collective-permute-start
  407.8 15.7 %all-reduce.2.cloned.1.call-done = bf16[32,1664]{1,0:T(8,128)(2,1)} async-done(((bf16[32,1664]{1,0:T(8,128)(2,1)}), bf16[32,1664]{1,0:T(8,128)(2,1)}) %all-reduce.2.cloned.1.call-update) | async-done | bytes 106512 | tf_op jit(solution)/shard_map/while/body/eval_jaxpr/psum | solution.py:108
  423.6 1.1 fusion.48
  424.7 1.1 bitcast_dynamic-update-slice_fusion.2
  425.8 1.3 collective-permute-start.1
  427.7 5.2 collective-permute-done.1
  434.1 1.0 convert_reduce_fusion.3
  436.2 7.9 %conditional.2 = (bf16[32,1664]{1,0:T(8,128)(2,1)S(1)}, bf16[32,3200]{1,0:T(8,128)(2,1)S(1)}, bf16[1,32,1664]{2,1,0:T(8,128)(2,1)S(1)}, bf16[1,32,3200]{2,1,0:T(8,128)(2,1)S(1)}) conditional(s32[]{:T(128)} %clamp.6, () %tuple.62, (bf16[32,1664]{1,0:T(8,128)(2,1)S(1)}, f32[1,1664]{1,0:T(1,128)}, bf16[1664,3200]{1,0:T(8,128)(2,1)}, ...), branch_computations={%region_1.1_spmd, %region_2.2_spmd, %region_3.5_spmd} | conditional | flops 343830560 | bytes 12458690 | solution.py:100
  436.2 7.1 %fusion.21 = bf16[32,1664]{1,0:T(8,128)(2,1)S(1)} fusion(bf16[1664,3200]{1,0:T(8,128)(2,1)} %get-tuple-element.187, bf16[32,3200]{1,0:T(8,128)(2,1)S(1)} %get-tuple-element.186, bf16[32,3200]{1,0:T(8,128)(2,1)S(1)} %get-tuple-element.185), kind=kOutput, calls=%fused_computation.33 | convolution fusion | flops 342016000 | bytes 11165696 | tf_op jit(solution)/shard_map/while/body/eval_jaxpr/cond/branch_2_fun/dot_general | solution.py:86
  444.8 1.3 collective-permute-start
  447.0 15.1 %all-reduce.2.cloned.1.call-done = bf16[32,1664]{1,0:T(8,128)(2,1)} async-done(((bf16[32,1664]{1,0:T(8,128)(2,1)}), bf16[32,1664]{1,0:T(8,128)(2,1)}) %all-reduce.2.cloned.1.call-update) | async-done | bytes 106512 | tf_op jit(solution)/shard_map/while/body/eval_jaxpr/psum | solution.py:108
  462.1 1.1 fusion.48
  463.2 1.1 bitcast_dynamic-update-slice_fusion.2
  464.3 1.3 collective-permute-start.1
  466.2 5.2 collective-permute-done.1
  471.4 8.0 %bitcast_convert_fusion = bf16[1664,3200]{1,0:T(8,128)(2,1)} fusion(bf16[5,32,1664]{2,1,0:T(8,128)(2,1)} %get-tuple-element.216, bf16[5,32,3200]{2,1,0:T(8,128)(2,1)S(1)} %get-tuple-element.217), kind=kOutput, calls=%fused_computation.59 | convolution fusion | flops 1368473600 | bytes 12001280 | tf_op jit(solution)/shard_map/dot_general | solution.py:137
  480.2 181.6 %reduce-scatter.2.cloned.1.call-done = bf16[416,3200]{1,0:T(8,128)(2,1)} async-done(((bf16[1664,3200]{1,0:T(8,128)(2,1)}), bf16[416,3200]{1,0:T(8,128)(2,1)}) %reduce-scatter.2.cloned.1.call-update) | async-done | bytes 2662416 | tf_op jit(solution)/shard_map/reduce_scatter | solution.py:136
  (170 shorter events, 31.5 us)
Async XLA Ops:
  7.2 191.7 %all-gather.3.cloned.1.call-start = ((), (), s32[]{:S(2)}) async-start(), calls=%async_computation.2 | async-start | bytes 13312000 | tf_op jit(solution)/shard_map/all_gather | solution.py:60
  199.9 27.0 %all-reduce.2.cloned.1.call-start = ((), (), s32[]{:S(2)}) async-start(), calls=%async_computation.3 | async-start | bytes 212992 | tf_op jit(solution)/shard_map/while/body/eval_jaxpr/psum | solution.py:108
  203.3 0.6 copy-start
  204.0 27.0 %collective-permute-start = (bf16[32,3200]{1,0:T(8,128)(2,1)S(1)}, bf16[32,3200]{1,0:T(8,128)(2,1)S(1)}, u32[]{:S(2)}, u32[]{:S(2)}) collective-permute-start(bf16[32,3200]{1,0:T(8,128)(2,1)S(1)} %get-tuple-element.378), channel_id=1, source_target_pairs={{8,0},{16,8},{24,16},{9,1},{17,9},{25,17},{10,2},{18,10},{26,18},{... | collective-permute-start | bytes 614408 | tf_op jit(solution)/shard_map/while/body/eval_jaxpr/ppermute | solution.py:22
  229.1 7.1 %collective-permute-start.1 = (bf16[32,1664]{1,0:T(8,128)(2,1)S(1)}, bf16[32,1664]{1,0:T(8,128)(2,1)S(1)}, u32[]{:S(2)}, u32[]{:S(2)}) collective-permute-start(bf16[32,1664]{1,0:T(8,128)(2,1)S(1)} %get-tuple-element.379), channel_id=1, source_target_pairs={{8,0},{16,8},{24,16},{9,1},{17,9},{25,17},{10,2},{18,10},{26,18},{... | collective-permute-start | bytes 319496 | tf_op jit(solution)/shard_map/while/body/eval_jaxpr/ppermute | solution.py:22
  236.2 30.1 %all-reduce.2.cloned.1.call-start = ((), (), s32[]{:S(2)}) async-start(), calls=%async_computation.3 | async-start | bytes 212992 | tf_op jit(solution)/shard_map/while/body/eval_jaxpr/psum | solution.py:108
  239.5 0.6 copy-start
  240.2 30.2 %collective-permute-start = (bf16[32,3200]{1,0:T(8,128)(2,1)S(1)}, bf16[32,3200]{1,0:T(8,128)(2,1)S(1)}, u32[]{:S(2)}, u32[]{:S(2)}) collective-permute-start(bf16[32,3200]{1,0:T(8,128)(2,1)S(1)} %get-tuple-element.378), channel_id=1, source_target_pairs={{8,0},{16,8},{24,16},{9,1},{17,9},{25,17},{10,2},{18,10},{26,18},{... | collective-permute-start | bytes 614408 | tf_op jit(solution)/shard_map/while/body/eval_jaxpr/ppermute | solution.py:22
  268.4 7.1 %collective-permute-start.1 = (bf16[32,1664]{1,0:T(8,128)(2,1)S(1)}, bf16[32,1664]{1,0:T(8,128)(2,1)S(1)}, u32[]{:S(2)}, u32[]{:S(2)}) collective-permute-start(bf16[32,1664]{1,0:T(8,128)(2,1)S(1)} %get-tuple-element.379), channel_id=1, source_target_pairs={{8,0},{16,8},{24,16},{9,1},{17,9},{25,17},{10,2},{18,10},{26,18},{... | collective-permute-start | bytes 319496 | tf_op jit(solution)/shard_map/while/body/eval_jaxpr/ppermute | solution.py:22
  275.6 30.1 %all-reduce.2.cloned.1.call-start = ((), (), s32[]{:S(2)}) async-start(), calls=%async_computation.3 | async-start | bytes 212992 | tf_op jit(solution)/shard_map/while/body/eval_jaxpr/psum | solution.py:108
  278.9 0.6 copy-start
  279.6 30.2 %collective-permute-start = (bf16[32,3200]{1,0:T(8,128)(2,1)S(1)}, bf16[32,3200]{1,0:T(8,128)(2,1)S(1)}, u32[]{:S(2)}, u32[]{:S(2)}) collective-permute-start(bf16[32,3200]{1,0:T(8,128)(2,1)S(1)} %get-tuple-element.378), channel_id=1, source_target_pairs={{8,0},{16,8},{24,16},{9,1},{17,9},{25,17},{10,2},{18,10},{26,18},{... | collective-permute-start | bytes 614408 | tf_op jit(solution)/shard_map/while/body/eval_jaxpr/ppermute | solution.py:22
  307.8 7.1 %collective-permute-start.1 = (bf16[32,1664]{1,0:T(8,128)(2,1)S(1)}, bf16[32,1664]{1,0:T(8,128)(2,1)S(1)}, u32[]{:S(2)}, u32[]{:S(2)}) collective-permute-start(bf16[32,1664]{1,0:T(8,128)(2,1)S(1)} %get-tuple-element.379), channel_id=1, source_target_pairs={{8,0},{16,8},{24,16},{9,1},{17,9},{25,17},{10,2},{18,10},{26,18},{... | collective-permute-start | bytes 319496 | tf_op jit(solution)/shard_map/while/body/eval_jaxpr/ppermute | solution.py:22
  314.9 30.1 %all-reduce.2.cloned.1.call-start = ((), (), s32[]{:S(2)}) async-start(), calls=%async_computation.3 | async-start | bytes 212992 | tf_op jit(solution)/shard_map/while/body/eval_jaxpr/psum | solution.py:108
  318.2 7.7 %copy-start.1 = (f32[1,1664]{1,0:T(1,128)S(1)}, f32[1,1664]{1,0:T(1,128)}, u32[]{:S(2)}) copy-start(f32[1,1664]{1,0:T(1,128)} %get-tuple-element.189) | copy-start | bytes 19972 | tf_op jit(solution)/shard_map/while/body/eval_jaxpr/cond
  326.1 0.6 copy-start
  326.8 22.4 %collective-permute-start = (bf16[32,3200]{1,0:T(8,128)(2,1)S(1)}, bf16[32,3200]{1,0:T(8,128)(2,1)S(1)}, u32[]{:S(2)}, u32[]{:S(2)}) collective-permute-start(bf16[32,3200]{1,0:T(8,128)(2,1)S(1)} %get-tuple-element.378), channel_id=1, source_target_pairs={{8,0},{16,8},{24,16},{9,1},{17,9},{25,17},{10,2},{18,10},{26,18},{... | collective-permute-start | bytes 614408 | tf_op jit(solution)/shard_map/while/body/eval_jaxpr/ppermute | solution.py:22
  347.2 7.1 %collective-permute-start.1 = (bf16[32,1664]{1,0:T(8,128)(2,1)S(1)}, bf16[32,1664]{1,0:T(8,128)(2,1)S(1)}, u32[]{:S(2)}, u32[]{:S(2)}) collective-permute-start(bf16[32,1664]{1,0:T(8,128)(2,1)S(1)} %get-tuple-element.379), channel_id=1, source_target_pairs={{8,0},{16,8},{24,16},{9,1},{17,9},{25,17},{10,2},{18,10},{26,18},{... | collective-permute-start | bytes 319496 | tf_op jit(solution)/shard_map/while/body/eval_jaxpr/ppermute | solution.py:22
  354.3 30.1 %all-reduce.2.cloned.1.call-start = ((), (), s32[]{:S(2)}) async-start(), calls=%async_computation.3 | async-start | bytes 212992 | tf_op jit(solution)/shard_map/while/body/eval_jaxpr/psum | solution.py:108
  357.6 7.7 %copy-start.1 = (f32[1,1664]{1,0:T(1,128)S(1)}, f32[1,1664]{1,0:T(1,128)}, u32[]{:S(2)}) copy-start(f32[1,1664]{1,0:T(1,128)} %get-tuple-element.189) | copy-start | bytes 19972 | tf_op jit(solution)/shard_map/while/body/eval_jaxpr/cond
  365.5 0.6 copy-start
  366.2 22.4 %collective-permute-start = (bf16[32,3200]{1,0:T(8,128)(2,1)S(1)}, bf16[32,3200]{1,0:T(8,128)(2,1)S(1)}, u32[]{:S(2)}, u32[]{:S(2)}) collective-permute-start(bf16[32,3200]{1,0:T(8,128)(2,1)S(1)} %get-tuple-element.378), channel_id=1, source_target_pairs={{8,0},{16,8},{24,16},{9,1},{17,9},{25,17},{10,2},{18,10},{26,18},{... | collective-permute-start | bytes 614408 | tf_op jit(solution)/shard_map/while/body/eval_jaxpr/ppermute | solution.py:22
  386.6 7.1 %collective-permute-start.1 = (bf16[32,1664]{1,0:T(8,128)(2,1)S(1)}, bf16[32,1664]{1,0:T(8,128)(2,1)S(1)}, u32[]{:S(2)}, u32[]{:S(2)}) collective-permute-start(bf16[32,1664]{1,0:T(8,128)(2,1)S(1)} %get-tuple-element.379), channel_id=1, source_target_pairs={{8,0},{16,8},{24,16},{9,1},{17,9},{25,17},{10,2},{18,10},{26,18},{... | collective-permute-start | bytes 319496 | tf_op jit(solution)/shard_map/while/body/eval_jaxpr/ppermute | solution.py:22
  393.7 29.9 %all-reduce.2.cloned.1.call-start = ((), (), s32[]{:S(2)}) async-start(), calls=%async_computation.3 | async-start | bytes 212992 | tf_op jit(solution)/shard_map/while/body/eval_jaxpr/psum | solution.py:108
  397.0 7.7 %copy-start.1 = (f32[1,1664]{1,0:T(1,128)S(1)}, f32[1,1664]{1,0:T(1,128)}, u32[]{:S(2)}) copy-start(f32[1,1664]{1,0:T(1,128)} %get-tuple-element.189) | copy-start | bytes 19972 | tf_op jit(solution)/shard_map/while/body/eval_jaxpr/cond
  404.9 0.6 copy-start
  405.6 22.2 %collective-permute-start = (bf16[32,3200]{1,0:T(8,128)(2,1)S(1)}, bf16[32,3200]{1,0:T(8,128)(2,1)S(1)}, u32[]{:S(2)}, u32[]{:S(2)}) collective-permute-start(bf16[32,3200]{1,0:T(8,128)(2,1)S(1)} %get-tuple-element.378), channel_id=1, source_target_pairs={{8,0},{16,8},{24,16},{9,1},{17,9},{25,17},{10,2},{18,10},{26,18},{... | collective-permute-start | bytes 614408 | tf_op jit(solution)/shard_map/while/body/eval_jaxpr/ppermute | solution.py:22
  425.8 7.1 %collective-permute-start.1 = (bf16[32,1664]{1,0:T(8,128)(2,1)S(1)}, bf16[32,1664]{1,0:T(8,128)(2,1)S(1)}, u32[]{:S(2)}, u32[]{:S(2)}) collective-permute-start(bf16[32,1664]{1,0:T(8,128)(2,1)S(1)} %get-tuple-element.379), channel_id=1, source_target_pairs={{8,0},{16,8},{24,16},{9,1},{17,9},{25,17},{10,2},{18,10},{26,18},{... | collective-permute-start | bytes 319496 | tf_op jit(solution)/shard_map/while/body/eval_jaxpr/ppermute | solution.py:22
  432.9 29.2 %all-reduce.2.cloned.1.call-start = ((), (), s32[]{:S(2)}) async-start(), calls=%async_computation.3 | async-start | bytes 212992 | tf_op jit(solution)/shard_map/while/body/eval_jaxpr/psum | solution.py:108
  436.2 7.7 %copy-start.1 = (f32[1,1664]{1,0:T(1,128)S(1)}, f32[1,1664]{1,0:T(1,128)}, u32[]{:S(2)}) copy-start(f32[1,1664]{1,0:T(1,128)} %get-tuple-element.189) | copy-start | bytes 19972 | tf_op jit(solution)/shard_map/while/body/eval_jaxpr/cond
  444.1 0.6 copy-start
  444.8 21.5 %collective-permute-start = (bf16[32,3200]{1,0:T(8,128)(2,1)S(1)}, bf16[32,3200]{1,0:T(8,128)(2,1)S(1)}, u32[]{:S(2)}, u32[]{:S(2)}) collective-permute-start(bf16[32,3200]{1,0:T(8,128)(2,1)S(1)} %get-tuple-element.378), channel_id=1, source_target_pairs={{8,0},{16,8},{24,16},{9,1},{17,9},{25,17},{10,2},{18,10},{26,18},{... | collective-permute-start | bytes 614408 | tf_op jit(solution)/shard_map/while/body/eval_jaxpr/ppermute | solution.py:22
  464.3 7.1 %collective-permute-start.1 = (bf16[32,1664]{1,0:T(8,128)(2,1)S(1)}, bf16[32,1664]{1,0:T(8,128)(2,1)S(1)}, u32[]{:S(2)}, u32[]{:S(2)}) collective-permute-start(bf16[32,1664]{1,0:T(8,128)(2,1)S(1)} %get-tuple-element.379), channel_id=1, source_target_pairs={{8,0},{16,8},{24,16},{9,1},{17,9},{25,17},{10,2},{18,10},{26,18},{... | collective-permute-start | bytes 319496 | tf_op jit(solution)/shard_map/while/body/eval_jaxpr/ppermute | solution.py:22
  471.4 190.4 %reduce-scatter.2.cloned.1.call-start = ((), (), s32[]{:S(2)}) async-start(), calls=%async_computation.1 | async-start | bytes 13312000 | tf_op jit(solution)/shard_map/reduce_scatter | solution.py:136
Sparse Core Ops, SparseCore 0:
  9.5 189.2 all-gather.2
  204.1 22.7 all-reduce.1
  240.3 25.8 all-reduce.1
  279.7 25.8 all-reduce.1
  326.9 18.0 all-reduce.1
  366.3 18.0 all-reduce.1
  405.7 17.8 all-reduce.1
  444.9 17.1 all-reduce.1
  479.5 182.1 reduce-scatter.1
where the time goes:
time: 670 us; the launch traced here: 668 us
  waiting for transfers between devices  538 us (80%)
  matrix products  37.9 us (6%)
  other arithmetic  32.5 us (5%)
  local copies, waits for them, and re-layouts  22 us (3%)
  starting transfers between devices  18.2 us (3%)
  between operations  13.8 us (2%)
    all_gather x1, waiting for transfers between devices, body(): full_weight = lax.all_gather(weights[0], 'dp', axis=0, tiled=True)  189 us
    reduce_scatter x1, waiting for transfers between devices, body(): lax.psum_scatter(lax.dot_general(flat_left, flat_right, (((0,), (0,)), ((...  182 us
    psum x7, waiting for transfers between devices, advance(): lax.psum(shortened(partial_value), 'tensor')  131 us
    ppermute x14, waiting for transfers between devices, shifted(): return lax.ppermute(block, axis, route)  36.1 us
    dot_general x4, matrix products, up_work(): lax.dot_general(act_grad, full_weight, (((1,), (1,)), ((), ())), preferre...  28.5 us
    ppermute x14, starting transfers between devices, shifted(): return lax.ppermute(block, axis, route)  18.1 us
  transfers between devices with their start and end apart: 23, of which 16 were waited for; matrix products, arithmetic and copies ran while one was open for 4% of the time, Pallas kernels for 0%

commit v1 on v0

--- a/solution.py
+++ b/solution.py
@@ -105,7 +105,8 @@
         inv_std = lax.rsqrt(jnp.mean(center * center, axis=-1, keepdims=True) + norm_eps)
         unit_rows = center * inv_std
         summed = jax.tree.map(
-            lambda part: part.astype(jnp.float32), lax.psum(shortened(partial_value), "tensor")
+            lambda part: part.astype(jnp.float32),
+            jnp.sum(lax.all_gather(shortened(partial_value), "tensor"), axis=0),
         )
         back_out = norm_back(incoming, summed, unit_rows, inv_std, channel_gain)
         outgoing = jnp.where(is_up, back_out, incoming)

time: 670 us -> 556 us (0.83)
  waiting for transfers between devices: 538 us -> 428 us
  blocking collectives: 0 us -> 13.7 us
  other arithmetic: 32.5 us -> 20.3 us
    psum x7 -> x0, waiting for transfers between devices: 131 us -> none  [advance(): lax.psum(shortened(partial_value), 'tensor')]
    ppermute x14, waiting for transfers between devices: 36.1 us -> 59.3 us  [shifted(): return lax.ppermute(block, axis, route)]
    all_gather x0 -> x7, blocking collectives: none -> 13.7 us  [advance(): lax.all_gather(shortened(partial_value), 'tensor')]
  transfers between devices with their start and end apart: 23 -> 16, of which waited for: 16 -> 9; matrix products, arithmetic and copies ran while one was open for 4% -> 3% of each run, Pallas kernels for 0% -> 0%
where the time goes in v1:
time: 556 us; the launch traced here: 554 us
  waiting for transfers between devices  428 us (77%)
  matrix products  37.9 us (7%)
  other arithmetic  20.3 us (4%)
  starting transfers between devices  18.2 us (3%)
  local copies, waits for them, and re-layouts  17.5 us (3%)
  between operations  14.1 us (3%)
  blocking collectives  13.7 us (2%)
    all_gather x1, waiting for transfers between devices, body(): full_weight = lax.all_gather(weights[0], 'dp', axis=0, tiled=True)  189 us
    reduce_scatter x1, waiting for transfers between devices, body(): lax.psum_scatter(lax.dot_general(flat_left, flat_right, (((0,), (0,)), ((...  179 us
    ppermute x14, waiting for transfers between devices, shifted(): return lax.ppermute(block, axis, route)  59.3 us
    dot_general x4, matrix products, up_work(): lax.dot_general(act_grad, full_weight, (((1,), (1,)), ((), ())), preferre...  28.5 us
    ppermute x14, starting transfers between devices, shifted(): return lax.ppermute(block, axis, route)  18.1 us
    all_gather x7, blocking collectives, advance(): lax.all_gather(shortened(partial_value), 'tensor')  13.7 us
  transfers between devices with their start and end apart: 16, of which 9 were waited for; matrix products, arithmetic and copies ran while one was open for 3% of the time, Pallas kernels for 0%

profile of v1, /device:TPU:0, one launch (start us, length us, event | category | flops | bytes accessed | tf_op | source)
XLA Modules:
  0.0 554.2 jit_solution(7590897585070284886)
XLA Ops:
  8.0 0.7 iota_compare_fusion.2
  8.7 1.3 convolution_convert_fusion.1
  10.0 188.8 %all-gather.6.cloned.1.call-done = bf16[1,1664,3200]{2,1,0:T(8,128)(2,1)} async-done(((bf16[1,416,3200]{2,1,0:T(8,128)(2,1)}), bf16[1,1664,3200]{2,1,0:T(8,128)(2,1)}) %all-gather.6.cloned.1.call-update) | async-done | bytes 10649616 | tf_op jit(solution)/shard_map/all_gather | solution.py:60
  199.0 0.8 broadcast.118
  199.9 159.8 %while.20 = (s32[]{:T(128)}, bf16[5,32,1664]{2,1,0:T(8,128)(2,1)}, bf16[5,32,3200]{2,1,0:T(8,128)(2,1)S(1)}, bf16[5,32,1664]{2,1,0:T(8,128)(2,1)S(1)}, bf16[32,3...) while((s32[]{:T(128)}, bf16[5,32,1664]{2,1,0:T(8,128)(2,1)}, ...), condition=%wide.region_11.12_spmd, body=%wide.region_0.11_spmd.sunk | while | flops 345374784 | bytes 16792116 | solution.py:132
  201.0 1.0 convert_reduce_fusion.3
  202.1 1.0 dynamic-slice_bitcast_fusion.4
  203.2 1.3 collective-permute-start
  204.5 0.7 reduce.8
  205.4 2.0 all-gather.3
  207.8 1.3 collective-permute-start.1
  209.8 5.8 %collective-permute-done.1 = bf16[32,1664]{1,0:T(8,128)(2,1)S(1)} collective-permute-done((bf16[32,1664]{1,0:T(8,128)(2,1)S(1)}, bf16[32,1664]{1,0:T(8,128)(2,1)S(1)}, u32[]{:S(2)}, u32[]{:S(2)}) %collective-permute-start.1) | collective-permute-done | bytes 106528 | tf_op jit(solution)/shard_map/while/body/eval_jaxpr/ppermute | solution.py:22
  216.8 1.0 convert_reduce_fusion.3
  217.8 1.0 dynamic-slice_bitcast_fusion.4
  218.9 1.3 collective-permute-start
  220.2 0.7 reduce.8
  221.2 2.0 all-gather.3
  223.5 1.3 collective-permute-start.1
  225.5 6.5 %collective-permute-done.1 = bf16[32,1664]{1,0:T(8,128)(2,1)S(1)} collective-permute-done((bf16[32,1664]{1,0:T(8,128)(2,1)S(1)}, bf16[32,1664]{1,0:T(8,128)(2,1)S(1)}, u32[]{:S(2)}, u32[]{:S(2)}) %collective-permute-start.1) | collective-permute-done | bytes 106528 | tf_op jit(solution)/shard_map/while/body/eval_jaxpr/ppermute | solution.py:22
  233.1 1.0 convert_reduce_fusion.3
  234.2 1.0 dynamic-slice_bitcast_fusion.4
  235.3 1.3 collective-permute-start
  236.6 0.7 reduce.8
  237.5 2.0 all-gather.3
  239.9 1.3 collective-permute-start.1
  241.9 23.6 %collective-permute-done.1 = bf16[32,1664]{1,0:T(8,128)(2,1)S(1)} collective-permute-done((bf16[32,1664]{1,0:T(8,128)(2,1)S(1)}, bf16[32,1664]{1,0:T(8,128)(2,1)S(1)}, u32[]{:S(2)}, u32[]{:S(2)}) %collective-permute-start.1) | collective-permute-done | bytes 106528 | tf_op jit(solution)/shard_map/while/body/eval_jaxpr/ppermute | solution.py:22
  266.6 1.0 convert_reduce_fusion.3
  267.7 1.0 dynamic-slice_bitcast_fusion.4
  268.7 7.9 %conditional.2 = (bf16[32,1664]{1,0:T(8,128)(2,1)S(1)}, bf16[32,3200]{1,0:T(8,128)(2,1)S(1)}, bf16[1,32,1664]{2,1,0:T(8,128)(2,1)S(1)}, bf16[1,32,3200]{2,1,0:T(8,128)(2,1)S(1)}) conditional(s32[]{:T(128)} %clamp.7, () %tuple.63, (bf16[32,1664]{1,0:T(8,128)(2,1)S(1)}, f32[1,1664]{1,0:T(1,128)}, bf16[1664,3200]{1,0:T(8,128)(2,1)}, ...), branch_computations={%region_1.1_spmd, %region_2.2_spmd, %region_3.5_spmd} | conditional | flops 343830560 | bytes 12458690 | solution.py:100
  268.7 7.1 %fusion.21 = bf16[32,1664]{1,0:T(8,128)(2,1)S(1)} fusion(bf16[1664,3200]{1,0:T(8,128)(2,1)} %get-tuple-element.205, bf16[32,3200]{1,0:T(8,128)(2,1)S(1)} %get-tuple-element.204, bf16[32,3200]{1,0:T(8,128)(2,1)S(1)} %get-tuple-element.203), kind=kOutput, calls=%fused_computation.33 | convolution fusion | flops 342016000 | bytes 11165696 | tf_op jit(solution)/shard_map/while/body/eval_jaxpr/cond/branch_2_fun/dot_general | solution.py:86
  276.6 1.3 collective-permute-start
  277.9 0.7 reduce.8
  278.8 2.0 all-gather.3
  281.2 1.3 collective-permute-start.1
  283.2 5.8 %collective-permute-done.1 = bf16[32,1664]{1,0:T(8,128)(2,1)S(1)} collective-permute-done((bf16[32,1664]{1,0:T(8,128)(2,1)S(1)}, bf16[32,1664]{1,0:T(8,128)(2,1)S(1)}, u32[]{:S(2)}, u32[]{:S(2)}) %collective-permute-start.1) | collective-permute-done | bytes 106528 | tf_op jit(solution)/shard_map/while/body/eval_jaxpr/ppermute | solution.py:22
  290.2 1.0 convert_reduce_fusion.3
  291.2 1.0 dynamic-slice_bitcast_fusion.4
  292.2 7.9 %conditional.2 = (bf16[32,1664]{1,0:T(8,128)(2,1)S(1)}, bf16[32,3200]{1,0:T(8,128)(2,1)S(1)}, bf16[1,32,1664]{2,1,0:T(8,128)(2,1)S(1)}, bf16[1,32,3200]{2,1,0:T(8,128)(2,1)S(1)}) conditional(s32[]{:T(128)} %clamp.7, () %tuple.63, (bf16[32,1664]{1,0:T(8,128)(2,1)S(1)}, f32[1,1664]{1,0:T(1,128)}, bf16[1664,3200]{1,0:T(8,128)(2,1)}, ...), branch_computations={%region_1.1_spmd, %region_2.2_spmd, %region_3.5_spmd} | conditional | flops 343830560 | bytes 12458690 | solution.py:100
  292.3 7.1 %fusion.21 = bf16[32,1664]{1,0:T(8,128)(2,1)S(1)} fusion(bf16[1664,3200]{1,0:T(8,128)(2,1)} %get-tuple-element.205, bf16[32,3200]{1,0:T(8,128)(2,1)S(1)} %get-tuple-element.204, bf16[32,3200]{1,0:T(8,128)(2,1)S(1)} %get-tuple-element.203), kind=kOutput, calls=%fused_computation.33 | convolution fusion | flops 342016000 | bytes 11165696 | tf_op jit(solution)/shard_map/while/body/eval_jaxpr/cond/branch_2_fun/dot_general | solution.py:86
  300.1 1.3 collective-permute-start
  301.4 0.7 reduce.8
  302.4 2.0 all-gather.3
  304.8 1.3 collective-permute-start.1
  306.8 5.8 %collective-permute-done.1 = bf16[32,1664]{1,0:T(8,128)(2,1)S(1)} collective-permute-done((bf16[32,1664]{1,0:T(8,128)(2,1)S(1)}, bf16[32,1664]{1,0:T(8,128)(2,1)S(1)}, u32[]{:S(2)}, u32[]{:S(2)}) %collective-permute-start.1) | collective-permute-done | bytes 106528 | tf_op jit(solution)/shard_map/while/body/eval_jaxpr/ppermute | solution.py:22
  313.7 1.0 convert_reduce_fusion.3
  314.8 1.0 dynamic-slice_bitcast_fusion.4
  315.8 7.9 %conditional.2 = (bf16[32,1664]{1,0:T(8,128)(2,1)S(1)}, bf16[32,3200]{1,0:T(8,128)(2,1)S(1)}, bf16[1,32,1664]{2,1,0:T(8,128)(2,1)S(1)}, bf16[1,32,3200]{2,1,0:T(8,128)(2,1)S(1)}) conditional(s32[]{:T(128)} %clamp.7, () %tuple.63, (bf16[32,1664]{1,0:T(8,128)(2,1)S(1)}, f32[1,1664]{1,0:T(1,128)}, bf16[1664,3200]{1,0:T(8,128)(2,1)}, ...), branch_computations={%region_1.1_spmd, %region_2.2_spmd, %region_3.5_spmd} | conditional | flops 343830560 | bytes 12458690 | solution.py:100
  315.8 7.1 %fusion.21 = bf16[32,1664]{1,0:T(8,128)(2,1)S(1)} fusion(bf16[1664,3200]{1,0:T(8,128)(2,1)} %get-tuple-element.205, bf16[32,3200]{1,0:T(8,128)(2,1)S(1)} %get-tuple-element.204, bf16[32,3200]{1,0:T(8,128)(2,1)S(1)} %get-tuple-element.203), kind=kOutput, calls=%fused_computation.33 | convolution fusion | flops 342016000 | bytes 11165696 | tf_op jit(solution)/shard_map/while/body/eval_jaxpr/cond/branch_2_fun/dot_general | solution.py:86
  323.7 1.3 collective-permute-start
  325.9 2.0 all-gather.3
  328.3 1.3 collective-permute-start.1
  330.3 5.8 %collective-permute-done.1 = bf16[32,1664]{1,0:T(8,128)(2,1)S(1)} collective-permute-done((bf16[32,1664]{1,0:T(8,128)(2,1)S(1)}, bf16[32,1664]{1,0:T(8,128)(2,1)S(1)}, u32[]{:S(2)}, u32[]{:S(2)}) %collective-permute-start.1) | collective-permute-done | bytes 106528 | tf_op jit(solution)/shard_map/while/body/eval_jaxpr/ppermute | solution.py:22
  337.3 1.0 convert_reduce_fusion.3
  338.3 1.0 dynamic-slice_bitcast_fusion.4
  339.3 7.9 %conditional.2 = (bf16[32,1664]{1,0:T(8,128)(2,1)S(1)}, bf16[32,3200]{1,0:T(8,128)(2,1)S(1)}, bf16[1,32,1664]{2,1,0:T(8,128)(2,1)S(1)}, bf16[1,32,3200]{2,1,0:T(8,128)(2,1)S(1)}) conditional(s32[]{:T(128)} %clamp.7, () %tuple.63, (bf16[32,1664]{1,0:T(8,128)(2,1)S(1)}, f32[1,1664]{1,0:T(1,128)}, bf16[1664,3200]{1,0:T(8,128)(2,1)}, ...), branch_computations={%region_1.1_spmd, %region_2.2_spmd, %region_3.5_spmd} | conditional | flops 343830560 | bytes 12458690 | solution.py:100
  339.4 7.1 %fusion.21 = bf16[32,1664]{1,0:T(8,128)(2,1)S(1)} fusion(bf16[1664,3200]{1,0:T(8,128)(2,1)} %get-tuple-element.205, bf16[32,3200]{1,0:T(8,128)(2,1)S(1)} %get-tuple-element.204, bf16[32,3200]{1,0:T(8,128)(2,1)S(1)} %get-tuple-element.203), kind=kOutput, calls=%fused_computation.33 | convolution fusion | flops 342016000 | bytes 11165696 | tf_op jit(solution)/shard_map/while/body/eval_jaxpr/cond/branch_2_fun/dot_general | solution.py:86
  347.2 1.3 collective-permute-start
  348.5 0.7 reduce.8
  349.5 2.0 all-gather.3
  351.9 1.3 collective-permute-start.1
  353.9 5.8 %collective-permute-done.1 = bf16[32,1664]{1,0:T(8,128)(2,1)S(1)} collective-permute-done((bf16[32,1664]{1,0:T(8,128)(2,1)S(1)}, bf16[32,1664]{1,0:T(8,128)(2,1)S(1)}, u32[]{:S(2)}, u32[]{:S(2)}) %collective-permute-start.1) | collective-permute-done | bytes 106528 | tf_op jit(solution)/shard_map/while/body/eval_jaxpr/ppermute | solution.py:22
  359.7 8.0 %bitcast_convert_fusion = bf16[1664,3200]{1,0:T(8,128)(2,1)} fusion(bf16[5,32,1664]{2,1,0:T(8,128)(2,1)} %get-tuple-element.234, bf16[5,32,3200]{2,1,0:T(8,128)(2,1)S(1)} %get-tuple-element.235), kind=kOutput, calls=%fused_computation.59 | convolution fusion | flops 1368473600 | bytes 12001280 | tf_op jit(solution)/shard_map/dot_general | solution.py:138
  367.7 0.8 slice_bitcast_fusion
  368.5 178.8 %reduce-scatter.2.cloned.1.call-done = bf16[416,3200]{1,0:T(8,128)(2,1)} async-done(((bf16[1664,3200]{1,0:T(8,128)(2,1)}), bf16[416,3200]{1,0:T(8,128)(2,1)}) %reduce-scatter.2.cloned.1.call-update) | async-done | bytes 2662416 | tf_op jit(solution)/shard_map/reduce_scatter | solution.py:137
  (149 shorter events, 18.4 us)
Async XLA Ops:
  7.2 191.7 %all-gather.6.cloned.1.call-start = ((), (), s32[]{:S(2)}) async-start(), calls=%async_computation.2 | async-start | bytes 13312000 | tf_op jit(solution)/shard_map/all_gather | solution.py:60
  7.9 539.5 %reduce-scatter.2.cloned.1.call-start = ((), (), s32[]{:S(2)}) async-start(), calls=%async_computation.1 | async-start | bytes 13312000 | tf_op jit(solution)/shard_map/reduce_scatter | solution.py:137
  203.2 12.5 %collective-permute-start = (bf16[32,3200]{1,0:T(8,128)(2,1)S(1)}, bf16[32,3200]{1,0:T(8,128)(2,1)S(1)}, u32[]{:S(2)}, u32[]{:S(2)}) collective-permute-start(bf16[32,3200]{1,0:T(8,128)(2,1)S(1)} %get-tuple-element.396), channel_id=1, source_target_pairs={{8,0},{16,8},{24,16},{9,1},{17,9},{25,17},{10,2},{18,10},{26,18},{... | collective-permute-start | bytes 614408 | tf_op jit(solution)/shard_map/while/body/eval_jaxpr/ppermute | solution.py:22
  207.8 7.8 %collective-permute-start.1 = (bf16[32,1664]{1,0:T(8,128)(2,1)S(1)}, bf16[32,1664]{1,0:T(8,128)(2,1)S(1)}, u32[]{:S(2)}, u32[]{:S(2)}) collective-permute-start(bf16[32,1664]{1,0:T(8,128)(2,1)S(1)} %get-tuple-element.397), channel_id=1, source_target_pairs={{8,0},{16,8},{24,16},{9,1},{17,9},{25,17},{10,2},{18,10},{26,18},{... | collective-permute-start | bytes 319496 | tf_op jit(solution)/shard_map/while/body/eval_jaxpr/ppermute | solution.py:22
  218.9 13.1 %collective-permute-start = (bf16[32,3200]{1,0:T(8,128)(2,1)S(1)}, bf16[32,3200]{1,0:T(8,128)(2,1)S(1)}, u32[]{:S(2)}, u32[]{:S(2)}) collective-permute-start(bf16[32,3200]{1,0:T(8,128)(2,1)S(1)} %get-tuple-element.396), channel_id=1, source_target_pairs={{8,0},{16,8},{24,16},{9,1},{17,9},{25,17},{10,2},{18,10},{26,18},{... | collective-permute-start | bytes 614408 | tf_op jit(solution)/shard_map/while/body/eval_jaxpr/ppermute | solution.py:22
  223.5 8.4 %collective-permute-start.1 = (bf16[32,1664]{1,0:T(8,128)(2,1)S(1)}, bf16[32,1664]{1,0:T(8,128)(2,1)S(1)}, u32[]{:S(2)}, u32[]{:S(2)}) collective-permute-start(bf16[32,1664]{1,0:T(8,128)(2,1)S(1)} %get-tuple-element.397), channel_id=1, source_target_pairs={{8,0},{16,8},{24,16},{9,1},{17,9},{25,17},{10,2},{18,10},{26,18},{... | collective-permute-start | bytes 319496 | tf_op jit(solution)/shard_map/while/body/eval_jaxpr/ppermute | solution.py:22
  235.3 30.2 %collective-permute-start = (bf16[32,3200]{1,0:T(8,128)(2,1)S(1)}, bf16[32,3200]{1,0:T(8,128)(2,1)S(1)}, u32[]{:S(2)}, u32[]{:S(2)}) collective-permute-start(bf16[32,3200]{1,0:T(8,128)(2,1)S(1)} %get-tuple-element.396), channel_id=1, source_target_pairs={{8,0},{16,8},{24,16},{9,1},{17,9},{25,17},{10,2},{18,10},{26,18},{... | collective-permute-start | bytes 614408 | tf_op jit(solution)/shard_map/while/body/eval_jaxpr/ppermute | solution.py:22
  239.9 25.6 %collective-permute-start.1 = (bf16[32,1664]{1,0:T(8,128)(2,1)S(1)}, bf16[32,1664]{1,0:T(8,128)(2,1)S(1)}, u32[]{:S(2)}, u32[]{:S(2)}) collective-permute-start(bf16[32,1664]{1,0:T(8,128)(2,1)S(1)} %get-tuple-element.397), channel_id=1, source_target_pairs={{8,0},{16,8},{24,16},{9,1},{17,9},{25,17},{10,2},{18,10},{26,18},{... | collective-permute-start | bytes 319496 | tf_op jit(solution)/shard_map/while/body/eval_jaxpr/ppermute | solution.py:22
  268.7 7.7 %copy-start = (f32[1,1664]{1,0:T(1,128)S(1)}, f32[1,1664]{1,0:T(1,128)}, u32[]{:S(2)}) copy-start(f32[1,1664]{1,0:T(1,128)} %get-tuple-element.207) | copy-start | bytes 19972 | tf_op jit(solution)/shard_map/while/body/eval_jaxpr/cond
  276.6 12.5 %collective-permute-start = (bf16[32,3200]{1,0:T(8,128)(2,1)S(1)}, bf16[32,3200]{1,0:T(8,128)(2,1)S(1)}, u32[]{:S(2)}, u32[]{:S(2)}) collective-permute-start(bf16[32,3200]{1,0:T(8,128)(2,1)S(1)} %get-tuple-element.396), channel_id=1, source_target_pairs={{8,0},{16,8},{24,16},{9,1},{17,9},{25,17},{10,2},{18,10},{26,18},{... | collective-permute-start | bytes 614408 | tf_op jit(solution)/shard_map/while/body/eval_jaxpr/ppermute | solution.py:22
  281.2 7.8 %collective-permute-start.1 = (bf16[32,1664]{1,0:T(8,128)(2,1)S(1)}, bf16[32,1664]{1,0:T(8,128)(2,1)S(1)}, u32[]{:S(2)}, u32[]{:S(2)}) collective-permute-start(bf16[32,1664]{1,0:T(8,128)(2,1)S(1)} %get-tuple-element.397), channel_id=1, source_target_pairs={{8,0},{16,8},{24,16},{9,1},{17,9},{25,17},{10,2},{18,10},{26,18},{... | collective-permute-start | bytes 319496 | tf_op jit(solution)/shard_map/while/body/eval_jaxpr/ppermute | solution.py:22
  292.2 7.7 %copy-start = (f32[1,1664]{1,0:T(1,128)S(1)}, f32[1,1664]{1,0:T(1,128)}, u32[]{:S(2)}) copy-start(f32[1,1664]{1,0:T(1,128)} %get-tuple-element.207) | copy-start | bytes 19972 | tf_op jit(solution)/shard_map/while/body/eval_jaxpr/cond
  300.1 12.5 %collective-permute-start = (bf16[32,3200]{1,0:T(8,128)(2,1)S(1)}, bf16[32,3200]{1,0:T(8,128)(2,1)S(1)}, u32[]{:S(2)}, u32[]{:S(2)}) collective-permute-start(bf16[32,3200]{1,0:T(8,128)(2,1)S(1)} %get-tuple-element.396), channel_id=1, source_target_pairs={{8,0},{16,8},{24,16},{9,1},{17,9},{25,17},{10,2},{18,10},{26,18},{... | collective-permute-start | bytes 614408 | tf_op jit(solution)/shard_map/while/body/eval_jaxpr/ppermute | solution.py:22
  304.8 7.8 %collective-permute-start.1 = (bf16[32,1664]{1,0:T(8,128)(2,1)S(1)}, bf16[32,1664]{1,0:T(8,128)(2,1)S(1)}, u32[]{:S(2)}, u32[]{:S(2)}) collective-permute-start(bf16[32,1664]{1,0:T(8,128)(2,1)S(1)} %get-tuple-element.397), channel_id=1, source_target_pairs={{8,0},{16,8},{24,16},{9,1},{17,9},{25,17},{10,2},{18,10},{26,18},{... | collective-permute-start | bytes 319496 | tf_op jit(solution)/shard_map/while/body/eval_jaxpr/ppermute | solution.py:22
  315.8 7.7 %copy-start = (f32[1,1664]{1,0:T(1,128)S(1)}, f32[1,1664]{1,0:T(1,128)}, u32[]{:S(2)}) copy-start(f32[1,1664]{1,0:T(1,128)} %get-tuple-element.207) | copy-start | bytes 19972 | tf_op jit(solution)/shard_map/while/body/eval_jaxpr/cond
  323.7 12.5 %collective-permute-start = (bf16[32,3200]{1,0:T(8,128)(2,1)S(1)}, bf16[32,3200]{1,0:T(8,128)(2,1)S(1)}, u32[]{:S(2)}, u32[]{:S(2)}) collective-permute-start(bf16[32,3200]{1,0:T(8,128)(2,1)S(1)} %get-tuple-element.396), channel_id=1, source_target_pairs={{8,0},{16,8},{24,16},{9,1},{17,9},{25,17},{10,2},{18,10},{26,18},{... | collective-permute-start | bytes 614408 | tf_op jit(solution)/shard_map/while/body/eval_jaxpr/ppermute | solution.py:22
  328.3 7.8 %collective-permute-start.1 = (bf16[32,1664]{1,0:T(8,128)(2,1)S(1)}, bf16[32,1664]{1,0:T(8,128)(2,1)S(1)}, u32[]{:S(2)}, u32[]{:S(2)}) collective-permute-start(bf16[32,1664]{1,0:T(8,128)(2,1)S(1)} %get-tuple-element.397), channel_id=1, source_target_pairs={{8,0},{16,8},{24,16},{9,1},{17,9},{25,17},{10,2},{18,10},{26,18},{... | collective-permute-start | bytes 319496 | tf_op jit(solution)/shard_map/while/body/eval_jaxpr/ppermute | solution.py:22
  339.4 7.7 %copy-start = (f32[1,1664]{1,0:T(1,128)S(1)}, f32[1,1664]{1,0:T(1,128)}, u32[]{:S(2)}) copy-start(f32[1,1664]{1,0:T(1,128)} %get-tuple-element.207) | copy-start | bytes 19972 | tf_op jit(solution)/shard_map/while/body/eval_jaxpr/cond
  347.2 12.5 %collective-permute-start = (bf16[32,3200]{1,0:T(8,128)(2,1)S(1)}, bf16[32,3200]{1,0:T(8,128)(2,1)S(1)}, u32[]{:S(2)}, u32[]{:S(2)}) collective-permute-start(bf16[32,3200]{1,0:T(8,128)(2,1)S(1)} %get-tuple-element.396), channel_id=1, source_target_pairs={{8,0},{16,8},{24,16},{9,1},{17,9},{25,17},{10,2},{18,10},{26,18},{... | collective-permute-start | bytes 614408 | tf_op jit(solution)/shard_map/while/body/eval_jaxpr/ppermute | solution.py:22
  351.9 7.8 %collective-permute-start.1 = (bf16[32,1664]{1,0:T(8,128)(2,1)S(1)}, bf16[32,1664]{1,0:T(8,128)(2,1)S(1)}, u32[]{:S(2)}, u32[]{:S(2)}) collective-permute-start(bf16[32,1664]{1,0:T(8,128)(2,1)S(1)} %get-tuple-element.397), channel_id=1, source_target_pairs={{8,0},{16,8},{24,16},{9,1},{17,9},{25,17},{10,2},{18,10},{26,18},{... | collective-permute-start | bytes 319496 | tf_op jit(solution)/shard_map/while/body/eval_jaxpr/ppermute | solution.py:22
Sparse Core Ops, SparseCore 0:
  9.5 189.2 all-gather.5
  367.9 179.4 reduce-scatter.1
